TPU v7x, 256 devices: a whole 4x4x8 slice. The times are simulated.
256 devices in a mesh: space: 16 (over z, core), mode: 16 (over y, x).
Axes of the slice: x: 4, y: 4, z: 8, core: 2. Of those that a mesh axis runs over, the one named last changes fastest.
Arguments:
- guess: float32 [8192, 2048], P('space', 'mode'), may hold values from -6 to 6
- forcing: float32 [8192, 2048], P('space', 'mode'), may hold values from -6 to 6
- spatial_diag: bfloat16 [8192, 512], P('space'), may hold values from -0.25 to 0.25
- spatial_ghost: bfloat16 [8192, 256], P('space'), may hold values from -0.375 to 0.375
- ghost_rows: int32 [32, 128], P('space'), may hold values from 0 to 511, as said below
- chaos_vals: bfloat16 [128, 128, 128], P('mode'), may hold values from -0.25 to 0.25
- chaos_targets: int32 [16, 8], replicated, may hold values from 0 to 15, as said below
- chaos_count: int32 [16], replicated, may hold values from 1 to 8, as said below
- mean_inverse: bfloat16 [2048, 2048], replicated, may hold values from -0.125 to 0.125
Outputs:
- field: float32 [8192, 2048], P('space', 'mode')
Inputs may be any that keep to these rules, and one draw needn't show every extreme that they name: `ghost_rows`: each row holds 128 distinct node numbers, 0 and 511 among them. `chaos_targets`: the targets in a row are distinct and the first is the row's own chaos block. Only the first chaos_count[j] slots of row j are used; some row uses all 8 slots and some row only one.
All inputs are finite; a program needn't handle non-finite values.
Results may differ from a plain program's by a relative error of at most 0.0021.
Values may be sent and summed in bfloat16 or wider, within the bound.
A program may use at most 128 MiB of HBM per device.

v0:
```python
import jax
import jax.numpy as jnp
from jax import lax
from jax.sharding import Mesh
from jax.sharding import PartitionSpec as P

ITERS = 3
SPACE = ("space_0", "space_1")
MODE = ("mode_0", "mode_1")
SPACE_MODE = ("space_0", "space_1", "mode_0", "mode_1")
step_gain = 0.5


def with_halo(cells, sides, width):
    for axis, dim in sides:
        count = lax.axis_size(axis)
        ends = count - 1
        head = lax.slice_in_dim(cells, 0, width, axis=dim)
        tail = lax.slice_in_dim(cells, cells.shape[dim] - width, cells.shape[dim], axis=dim)
        cells = jnp.concatenate(
            [
                lax.ppermute(tail, axis, [(i, (i + 1) % count) for i in range(ends)]),
                cells,
                lax.ppermute(head, axis, [((i + 1) % count, i) for i in range(ends)]),
            ],
            axis=dim,
        )
    return cells


def one_axis_at_a_time(value, axes):
    for axis in axes:
        value = lax.psum(value, axis)
    return value


def shards(
    guess,
    forcing,
    spatial_diag,
    spatial_ghost,
    ghost_rows,
    chaos_vals,
    chaos_targets,
    chaos_count,
    mean_inverse,
):
    node_rows, local_modes = guess.shape
    ghost_width = ghost_rows.shape[1]
    block_width = chaos_vals.shape[1]
    list_slots = chaos_targets.shape[1]
    all_blocks = chaos_targets.shape[0]
    total_cells = node_rows * lax.axis_size(SPACE) * local_modes * lax.axis_size(MODE)
    slab_tables = lax.all_gather(chaos_vals, MODE, axis=0, tiled=True)
    slab_tables = slab_tables.reshape(all_blocks, list_slots, block_width, block_width)
    slot_used = jnp.arange(list_slots, dtype=jnp.int32)[None, :] < chaos_count[:, None]
    every_block = jnp.arange(all_blocks, dtype=jnp.int32)
    target_hits = (chaos_targets[:, :, None] == every_block[None, None, :]) & slot_used[:, :, None]
    target_hits = target_hits.astype(jnp.bfloat16)
    full_table = jnp.einsum(
        "jsba,jst->jatb", slab_tables, target_hits, preferred_element_type=jnp.float32
    )
    full_table = full_table.astype(jnp.bfloat16).reshape(
        all_blocks * block_width, all_blocks * block_width
    )
    field = guess
    for iteration in range(ITERS):
        field_bf = field.astype(jnp.bfloat16)
        lower_sent = field_bf[ghost_rows[0]]
        upper_sent = field_bf[ghost_rows[1]]
        padded = with_halo(
            jnp.concatenate([lower_sent, upper_sent], axis=0), ((SPACE, 0),), ghost_width
        )
        ghosts = jnp.concatenate([padded[:ghost_width], padded[3 * ghost_width :]], axis=0)
        spatial = jnp.dot(spatial_diag, field_bf, preferred_element_type=jnp.float32)
        spatial = spatial + jnp.dot(spatial_ghost, ghosts, preferred_element_type=jnp.float32)
        field_slab = lax.all_to_all(field_bf, MODE, split_axis=0, concat_axis=1, tiled=True)
        partial_slab = lax.all_to_all(
            forcing - spatial, MODE, split_axis=0, concat_axis=1, tiled=True
        )
        coupled_slab = jnp.dot(field_slab, full_table, preferred_element_type=jnp.float32)
        residual_slab = (partial_slab - coupled_slab).astype(jnp.bfloat16)
        update_slab = lax.dot_general(
            residual_slab,
            mean_inverse,
            (((1,), (1,)), ((), ())),
            preferred_element_type=jnp.float32,
        )
        update = lax.all_to_all(update_slab, MODE, split_axis=1, concat_axis=0, tiled=True)
        squares = one_axis_at_a_time(jnp.sum(update * update), SPACE_MODE)
        damping = step_gain / jnp.sqrt(squares / total_cells + 1e-06)
        field = field + damping * update
    return field


def solution(mesh):
    torus = Mesh(mesh.devices.reshape(8, 2, 4, 4), ("space_0", "space_1", "mode_0", "mode_1"))
    in_specs = (
        P(SPACE, MODE),
        P(SPACE, MODE),
        P(SPACE, None),
        P(SPACE, None),
        P(SPACE, None),
        P(MODE, None, None),
        P(),
        P(),
        P(),
    )
    out_specs = P(SPACE, MODE)
    return jax.shard_map(
        shards, mesh=torus, in_specs=in_specs, out_specs=out_specs, check_vma=False
    )
```

profile of v0, /device:TPU:2, one launch (start us, length us, event | category | flops | bytes accessed | tf_op | source)
XLA Modules:
  0.0 349.0 jit_solution(4169821131279760908)
XLA Ops:
  17.1 7.5 %all-to-all-start.1 = ((bf16[16,32,128]{2,1,0:T(8,128)(2,1)}), bf16[16,32,128]{2,1,0:T(8,128)(2,1)S(1)}, u32[]{:S(2)}, u32[]{:S(2)}) async-start(bf16[16,32,128]{2,1,0:T(8,128)(2,1)} %bitcast.11), calls=%async_computation.1 | async-start | bytes 262144 | tf_op jit(solution)/shard_map/all_to_all | solution.py:77
  32.7 5.0 %all-to-all-start = ((f32[16,32,128]{2,1,0:T(8,128)}), f32[16,32,128]{2,1,0:T(8,128)S(1)}, u32[]{:S(2)}, u32[]{:S(2)}) async-start(f32[16,32,128]{2,1,0:T(8,128)} %bitcast.5), calls=%async_computation | async-start | bytes 524288 | tf_op jit(solution)/shard_map/all_to_all | solution.py:78
  37.7 32.6 %all-gather.2.cloned.1.call-done = bf16[128,128,128]{2,1,0:T(8,128)(2,1)} async-done(((bf16[8,128,128]{2,1,0:T(8,128)(2,1)}), bf16[128,128,128]{2,1,0:T(8,128)(2,1)}) %all-gather.2.cloned.1.call-update) | async-done | bytes 4194320 | tf_op jit(solution)/shard_map/all_gather | solution.py:54
  70.3 7.5 %convert_bitcast_fusion = bf16[16,128,16,128]{1,2,3,0:T(8,128)(2,1)} fusion(bf16[16,8,128,128]{3,2,1,0:T(8,128)(2,1)} %bitcast.187, s32[16,8]{1,0:T(8,128)S(1)} %copy.36, pred[16,8]{1,0:T(8,128)(4,1)S(1)} %iota_compare_fusion.1), kind=kOutput, calls=%fused_computation.12 | convolution fusion | flops 71307264 | bytes 12583552 | tf_op jit(solution)/shard_map/jsba,jst->jatb/dot_general | solution.py:60
  77.8 13.3 %copy.38 = bf16[16,128,16,128]{3,2,1,0:T(8,128)(2,1)} copy(bf16[16,128,16,128]{1,2,3,0:T(8,128)(2,1)} %convert_bitcast_fusion) | data formatting | bytes 16777216 | tf_op jit(solution)/shard_map/convert_element_type | solution.py:63
  91.1 9.8 %convolution_bitcast_fusion.2 = f32[4,16,8,128]{3,2,1,0:T(8,128)S(1)} fusion(bf16[2048,2048]{1,0:T(8,128)(2,1)} %param.17, bf16[256,8,16,128]{3,2,1,0:T(8,128)(2,1)} %bitcast.184, f32[16,32,128]{2,1,0:T(8,128)S(1)} %all-to-all-done, bf16[16,32,128]{2,1,0:T(8,128)(2,1)S(1)} %all-to-all-done.1), kind=kOutput, calls=%fused_computation.32 | convolution fusion | flops 537001984 | bytes 17432576 | tf_op jit(solution)/shard_map/dot_general | solution.py:83
  101.0 12.8 %all_to_all.153 = f32[32,16,128]{2,0,1:T(8,128)S(1)} all-to-all(f32[32,16,128]{2,0,1:T(8,128)S(1)} %bitcast.190), channel_id=1, replica_groups=mesh['space_0'=8,'space_1'=2,'mode_0'=4,'mode_1'=4] {'mode_0','mode_1'}, dimensions={1} | all-to-all | bytes 524288 | tf_op jit(solution)/shard_map/all_to_all | solution.py:89
  114.5 18.1 %psum.84 = f32[]{:T(128)} all-reduce(f32[]{:T(128)} %multiply_reduce_fusion.2), channel_id=1, replica_groups=mesh['space_0'=8,'space_1'=2,'mode_0'=4,'mode_1'=4] {'space_0'}, use_global_device_ids=true, to_apply=%region_1.0 | all-reduce | flops 1 | bytes 8 | tf_op jit(solution)/shard_map/psum | solution.py:33
  135.7 9.2 %psum.86 = f32[]{:T(128)} all-reduce(f32[]{:T(128)} %psum.85), channel_id=1, replica_groups=mesh['space_0'=8,'space_1'=2,'mode_0'=4,'mode_1'=4] {'mode_0'}, use_global_device_ids=true, to_apply=%region_3.0 | all-reduce | flops 1 | bytes 8 | tf_op jit(solution)/shard_map/psum | solution.py:33
  145.0 9.8 %psum.87 = f32[]{:T(128)} all-reduce(f32[]{:T(128)} %psum.86), channel_id=1, replica_groups=mesh['space_0'=8,'space_1'=2,'mode_0'=4,'mode_1'=4] {'mode_1'}, use_global_device_ids=true, to_apply=%region_4.0 | all-reduce | flops 1 | bytes 8 | tf_op jit(solution)/shard_map/psum | solution.py:33
  169.7 6.3 %all-to-all-done.4 = bf16[16,32,128]{2,1,0:T(8,128)(2,1)S(1)} async-done(((bf16[16,32,128]{2,1,0:T(8,128)(2,1)}), bf16[16,32,128]{2,1,0:T(8,128)(2,1)S(1)}, u32[]{:S(2)}, u32[]{:S(2)}) %all-to-all-start.4) | async-done | bytes 131104 | tf_op jit(solution)/shard_map/all_to_all | solution.py:77
  176.0 11.8 %all_to_all.154 = f32[16,32,128]{2,1,0:T(8,128)S(1)} all-to-all(f32[16,32,128]{2,1,0:T(8,128)S(1)} %bitcast.188), channel_id=1, replica_groups=mesh['space_0'=8,'space_1'=2,'mode_0'=4,'mode_1'=4] {'mode_0','mode_1'}, dimensions={0} | all-to-all | bytes 524288 | tf_op jit(solution)/shard_map/all_to_all | solution.py:78
  187.7 9.8 %convolution_bitcast_fusion.1 = f32[4,16,8,128]{3,2,1,0:T(8,128)S(1)} fusion(bf16[2048,2048]{1,0:T(8,128)(2,1)} %param.17, bf16[256,8,16,128]{3,2,1,0:T(8,128)(2,1)} %bitcast.185, f32[16,32,128]{2,1,0:T(8,128)S(1)} %all_to_all.154, bf16[16,32,128]{2,1,0:T(8,128)(2,1)S(1)} %all-to-all-done.4), kind=kOutput, calls=%fused_computation.28 | convolution fusion | flops 537001984 | bytes 17432576 | tf_op jit(solution)/shard_map/dot_general | solution.py:83
  197.5 11.6 %all_to_all.155 = f32[32,16,128]{2,0,1:T(8,128)S(1)} all-to-all(f32[32,16,128]{2,0,1:T(8,128)S(1)} %bitcast.191), channel_id=1, replica_groups=mesh['space_0'=8,'space_1'=2,'mode_0'=4,'mode_1'=4] {'mode_0','mode_1'}, dimensions={1} | all-to-all | bytes 524288 | tf_op jit(solution)/shard_map/all_to_all | solution.py:89
  209.8 15.6 %psum.88 = f32[]{:T(128)} all-reduce(f32[]{:T(128)} %multiply_reduce_fusion.1), channel_id=1, replica_groups=mesh['space_0'=8,'space_1'=2,'mode_0'=4,'mode_1'=4] {'space_0'}, use_global_device_ids=true, to_apply=%region_6.0 | all-reduce | flops 1 | bytes 8 | tf_op jit(solution)/shard_map/psum | solution.py:33
  228.5 9.2 %psum.90 = f32[]{:T(128)} all-reduce(f32[]{:T(128)} %psum.89), channel_id=1, replica_groups=mesh['space_0'=8,'space_1'=2,'mode_0'=4,'mode_1'=4] {'mode_0'}, use_global_device_ids=true, to_apply=%region_8.0 | all-reduce | flops 1 | bytes 8 | tf_op jit(solution)/shard_map/psum | solution.py:33
  237.7 9.8 %psum.91 = f32[]{:T(128)} all-reduce(f32[]{:T(128)} %psum.90), channel_id=1, replica_groups=mesh['space_0'=8,'space_1'=2,'mode_0'=4,'mode_1'=4] {'mode_1'}, use_global_device_ids=true, to_apply=%region_9.0 | all-reduce | flops 1 | bytes 8 | tf_op jit(solution)/shard_map/psum | solution.py:33
  262.3 6.8 %all-to-all-done.7 = bf16[16,32,128]{2,1,0:T(8,128)(2,1)S(1)} async-done(((bf16[16,32,128]{2,1,0:T(8,128)(2,1)}), bf16[16,32,128]{2,1,0:T(8,128)(2,1)S(1)}, u32[]{:S(2)}, u32[]{:S(2)}) %all-to-all-start.7) | async-done | bytes 131104 | tf_op jit(solution)/shard_map/all_to_all | solution.py:77
  269.1 11.8 %all_to_all.156 = f32[16,32,128]{2,1,0:T(8,128)S(1)} all-to-all(f32[16,32,128]{2,1,0:T(8,128)S(1)} %bitcast.189), channel_id=1, replica_groups=mesh['space_0'=8,'space_1'=2,'mode_0'=4,'mode_1'=4] {'mode_0','mode_1'}, dimensions={0} | all-to-all | bytes 524288 | tf_op jit(solution)/shard_map/all_to_all | solution.py:78
  280.9 9.8 %convolution_bitcast_fusion = f32[4,16,8,128]{3,2,1,0:T(8,128)S(1)} fusion(bf16[2048,2048]{1,0:T(8,128)(2,1)} %param.17, bf16[256,8,16,128]{3,2,1,0:T(8,128)(2,1)} %bitcast.186, f32[16,32,128]{2,1,0:T(8,128)S(1)} %all_to_all.156, bf16[16,32,128]{2,1,0:T(8,128)(2,1)S(1)} %all-to-all-done.7), kind=kOutput, calls=%fused_computation.24 | convolution fusion | flops 537001984 | bytes 17432576 | tf_op jit(solution)/shard_map/dot_general | solution.py:83
  290.7 11.6 %all_to_all.157 = f32[32,16,128]{2,0,1:T(8,128)S(1)} all-to-all(f32[32,16,128]{2,0,1:T(8,128)S(1)} %bitcast.192), channel_id=1, replica_groups=mesh['space_0'=8,'space_1'=2,'mode_0'=4,'mode_1'=4] {'mode_0','mode_1'}, dimensions={1} | all-to-all | bytes 524288 | tf_op jit(solution)/shard_map/all_to_all | solution.py:89
  302.9 15.7 %psum.92 = f32[]{:T(128)} all-reduce(f32[]{:T(128)} %multiply_reduce_fusion), channel_id=1, replica_groups=mesh['space_0'=8,'space_1'=2,'mode_0'=4,'mode_1'=4] {'space_0'}, use_global_device_ids=true, to_apply=%region_11.0 | all-reduce | flops 1 | bytes 8 | tf_op jit(solution)/shard_map/psum | solution.py:33
  321.7 9.2 %psum.94 = f32[]{:T(128)} all-reduce(f32[]{:T(128)} %psum.93), channel_id=1, replica_groups=mesh['space_0'=8,'space_1'=2,'mode_0'=4,'mode_1'=4] {'mode_0'}, use_global_device_ids=true, to_apply=%region_13.0 | all-reduce | flops 1 | bytes 8 | tf_op jit(solution)/shard_map/psum | solution.py:33
  330.9 9.8 %psum.95 = f32[]{:T(128)} all-reduce(f32[]{:T(128)} %psum.94), channel_id=1, replica_groups=mesh['space_0'=8,'space_1'=2,'mode_0'=4,'mode_1'=4] {'mode_1'}, use_global_device_ids=true, to_apply=%region_14.0 | all-reduce | flops 1 | bytes 8 | tf_op jit(solution)/shard_map/psum | solution.py:33
  (62 shorter events, 58.9 us)
Async XLA Ops:
  6.5 18.1 %copy-start = (bf16[512,512]{1,0:T(8,128)(2,1)S(1)}, bf16[512,512]{1,0:T(8,128)(2,1)}, u32[]{:S(2)}) copy-start(bf16[512,512]{1,0:T(8,128)(2,1)} %param.11) | copy-start | bytes 1572868
  6.5 63.8 %all-gather.2.cloned.1.call-start = ((), (), s32[]{:S(2)}) async-start(), calls=%async_computation.9 | async-start | bytes 4456448 | tf_op jit(solution)/shard_map/all_gather | solution.py:54
  11.2 16.1 %collective-permute-start.1 = (bf16[128,128]{1,0:T(8,128)(2,1)S(1)}, bf16[128,128]{1,0:T(8,128)(2,1)S(1)}, u32[]{:S(2)}, u32[]{:S(2)}) collective-permute-start(bf16[128,128]{1,0:T(8,128)(2,1)S(1)} %gather_fusion.1), channel_id=1, source_target_pairs={{16,0},{32,16},{48,32},{64,48},{80,64},{96,80},{112,96},{128,112},... | collective-permute-start | bytes 98312 | tf_op jit(solution)/shard_map/ppermute | solution.py:24
  14.1 13.3 %collective-permute-start = (bf16[128,128]{1,0:T(8,128)(2,1)S(1)}, bf16[128,128]{1,0:T(8,128)(2,1)S(1)}, u32[]{:S(2)}, u32[]{:S(2)}) collective-permute-start(bf16[128,128]{1,0:T(8,128)(2,1)S(1)} %gather_fusion), channel_id=1, source_target_pairs={{0,16},{16,32},{32,48},{48,64},{64,80},{80,96},{96,112},{112,128},... | collective-permute-start | bytes 98312 | tf_op jit(solution)/shard_map/ppermute | solution.py:22
  17.1 15.6 %all-to-all-start.1 = ((bf16[16,32,128]{2,1,0:T(8,128)(2,1)}), bf16[16,32,128]{2,1,0:T(8,128)(2,1)S(1)}, u32[]{:S(2)}, u32[]{:S(2)}) async-start(bf16[16,32,128]{2,1,0:T(8,128)(2,1)} %bitcast.11), calls=%async_computation.1 | async-start | bytes 262144 | tf_op jit(solution)/shard_map/all_to_all | solution.py:77
  32.7 58.5 %all-to-all-start = ((f32[16,32,128]{2,1,0:T(8,128)}), f32[16,32,128]{2,1,0:T(8,128)S(1)}, u32[]{:S(2)}, u32[]{:S(2)}) async-start(f32[16,32,128]{2,1,0:T(8,128)} %bitcast.5), calls=%async_computation | async-start | bytes 524288 | tf_op jit(solution)/shard_map/all_to_all | solution.py:78
  91.1 53.8 %copy-start.3 = (f32[512,128]{1,0:T(8,128)S(1)}, f32[512,128]{1,0:T(8,128)}, u32[]{:S(2)}) copy-start(f32[512,128]{1,0:T(8,128)} %param.10) | copy-start | bytes 786436
  91.1 64.4 %copy-start.1 = (f32[512,128]{1,0:T(8,128)S(1)}, f32[512,128]{1,0:T(8,128)}, u32[]{:S(2)}) copy-start(f32[512,128]{1,0:T(8,128)} %param.9) | copy-start | bytes 786436
  91.1 78.2 %copy-start.2 = (bf16[512,256]{1,0:T(8,128)(2,1)S(1)}, bf16[512,256]{1,0:T(8,128)(2,1)}, u32[]{:S(2)}) copy-start(bf16[512,256]{1,0:T(8,128)(2,1)} %param.12) | copy-start | bytes 786436
  159.4 9.9 %collective-permute-start.3 = (bf16[128,128]{1,0:T(8,128)(2,1)S(1)}, bf16[128,128]{1,0:T(8,128)(2,1)S(1)}, u32[]{:S(2)}, u32[]{:S(2)}) collective-permute-start(bf16[128,128]{1,0:T(8,128)(2,1)S(1)} %gather_fusion.3), channel_id=1, source_target_pairs={{16,0},{32,16},{48,32},{64,48},{80,64},{96,80},{112,96},{128,112},... | collective-permute-start | bytes 98312 | tf_op jit(solution)/shard_map/ppermute | solution.py:24
  160.7 8.6 %collective-permute-start.2 = (bf16[128,128]{1,0:T(8,128)(2,1)S(1)}, bf16[128,128]{1,0:T(8,128)(2,1)S(1)}, u32[]{:S(2)}, u32[]{:S(2)}) collective-permute-start(bf16[128,128]{1,0:T(8,128)(2,1)S(1)} %gather_fusion.2), channel_id=1, source_target_pairs={{0,16},{16,32},{32,48},{48,64},{64,80},{80,96},{96,112},{112,128},... | collective-permute-start | bytes 98312 | tf_op jit(solution)/shard_map/ppermute | solution.py:22
  165.0 11.0 %all-to-all-start.4 = ((bf16[16,32,128]{2,1,0:T(8,128)(2,1)}), bf16[16,32,128]{2,1,0:T(8,128)(2,1)S(1)}, u32[]{:S(2)}, u32[]{:S(2)}) async-start(bf16[16,32,128]{2,1,0:T(8,128)(2,1)} %bitcast.19), calls=%async_computation.4 | async-start | bytes 262144 | tf_op jit(solution)/shard_map/all_to_all | solution.py:77
  252.1 9.9 %collective-permute-start.5 = (bf16[128,128]{1,0:T(8,128)(2,1)S(1)}, bf16[128,128]{1,0:T(8,128)(2,1)S(1)}, u32[]{:S(2)}, u32[]{:S(2)}) collective-permute-start(bf16[128,128]{1,0:T(8,128)(2,1)S(1)} %gather_fusion.5), channel_id=1, source_target_pairs={{16,0},{32,16},{48,32},{64,48},{80,64},{96,80},{112,96},{128,112},... | collective-permute-start | bytes 98312 | tf_op jit(solution)/shard_map/ppermute | solution.py:24
  253.3 8.6 %collective-permute-start.4 = (bf16[128,128]{1,0:T(8,128)(2,1)S(1)}, bf16[128,128]{1,0:T(8,128)(2,1)S(1)}, u32[]{:S(2)}, u32[]{:S(2)}) collective-permute-start(bf16[128,128]{1,0:T(8,128)(2,1)S(1)} %gather_fusion.4), channel_id=1, source_target_pairs={{0,16},{16,32},{32,48},{48,64},{64,80},{80,96},{96,112},{112,128},... | collective-permute-start | bytes 98312 | tf_op jit(solution)/shard_map/ppermute | solution.py:22
  257.6 11.5 %all-to-all-start.7 = ((bf16[16,32,128]{2,1,0:T(8,128)(2,1)}), bf16[16,32,128]{2,1,0:T(8,128)(2,1)S(1)}, u32[]{:S(2)}, u32[]{:S(2)}) async-start(bf16[16,32,128]{2,1,0:T(8,128)(2,1)} %bitcast.26), calls=%async_computation.7 | async-start | bytes 262144 | tf_op jit(solution)/shard_map/all_to_all | solution.py:77
Sparse Core Ops, SparseCore 0:
  9.8 60.4 all-gather.1
where the time goes:
time: 351 us; the launch traced here: 349 us
  blocking collectives  175 us (50%)
  waiting for transfers between devices  49.9 us (14%)
  matrix products  42.9 us (12%)
  starting transfers between devices  34.1 us (10%)
  local copies, waits for them, and re-layouts  24 us (7%)
  between operations  15.7 us (4%)
  other arithmetic  7.31 us (2%)
    psum x12, blocking collectives, one_axis_at_a_time(): value = lax.psum(value, axis)  116 us
    all_to_all x3, blocking collectives, shards(): lax.all_to_all(update_slab, MODE, split_axis=1, concat_axis=0, tiled=True)  36 us
    all_gather x1, waiting for transfers between devices, shards(): slab_tables = lax.all_gather(chaos_vals, MODE, axis=0, tiled=True)  32.6 us
    dot_general x3, matrix products, shards(): lax.dot_general(residual_slab, mean_inverse, (((1,), (1,)), ((), ())), pr...  29.3 us
    all_to_all x2, blocking collectives, shards(): lax.all_to_all(forcing - spatial, MODE, split_axis=0, concat_axis=1, tile...  23.5 us
    all_to_all x3, waiting for transfers between devices, shards(): lax.all_to_all(field_bf, MODE, split_axis=0, concat_axis=1, tiled=True)  16.5 us
    all_to_all x3, starting transfers between devices, shards(): lax.all_to_all(field_bf, MODE, split_axis=0, concat_axis=1, tiled=True)  16.1 us
    convert_element_type x1, local copies, waits for them, and re-layouts, shards(): full_table.astype(jnp.bfloat16)  13.3 us
  transfers between devices with their start and end apart: 11, of which 4 were waited for; matrix products, arithmetic and copies ran while one was open for 10% of the time, Pallas kernels for 0%

commit v1 on v0

--- a/solution.py
+++ b/solution.py
@@ -30,7 +30,7 @@
 
 def one_axis_at_a_time(value, axes):
     for axis in axes:
-        value = lax.psum(value, axis)
+        value = jnp.sum(lax.all_gather(value, axis), axis=0)
     return value
 
 

time: 351 us -> 369 us (1.051)
  blocking collectives: 175 us -> 155 us
  local copies, waits for them, and re-layouts: 24 us -> 43.3 us
  other arithmetic: 7.31 us -> 14.6 us
  waiting for transfers between devices: 49.9 us -> 56.5 us
  starting transfers between devices: 34.1 us -> 39.8 us
    psum x12 -> x0, blocking collectives: 116 us -> none  [one_axis_at_a_time(): value = lax.psum(value, axis)]
    unnamed x0 -> x12, blocking collectives: none -> 108 us
    unnamed x10 -> x46, local copies, waits for them, and re-layouts: 0.9 us -> 19.5 us
    all_to_all x3 -> x2, blocking collectives: 36 us -> 23.2 us  [shards(): lax.all_to_all(update_slab, MODE, split_axis=1, concat_axis=0, tiled=True)]
    reduce_sum x0 -> x12, other arithmetic: none -> 7.24 us  [one_axis_at_a_time(): value = jnp.sum(lax.all_gather(value, axis), axis=0)]
    all_to_all x0 -> x1, waiting for transfers between devices: none -> 6.62 us  [shards(): lax.all_to_all(update_slab, MODE, split_axis=1, concat_axis=0, tiled=True)]
    all_to_all x0 -> x1, starting transfers between devices: none -> 5.72 us  [shards(): lax.all_to_all(update_slab, MODE, split_axis=1, concat_axis=0, tiled=True)]
  transfers between devices with their start and end apart: 11 -> 12, of which waited for: 4 -> 5; matrix products, arithmetic and copies ran while one was open for 10% -> 9% of each run, Pallas kernels for 0% -> 0%
where the time goes in v1:
time: 369 us; the launch traced here: 367 us
  blocking collectives  155 us (42%)
  waiting for transfers between devices  56.5 us (15%)
  local copies, waits for them, and re-layouts  43.3 us (12%)
  matrix products  42.9 us (12%)
  starting transfers between devices  39.8 us (11%)
  between operations  15.8 us (4%)
  other arithmetic  14.6 us (4%)
    unnamed x12, blocking collectives  108 us
    all_gather x1, waiting for transfers between devices, shards(): slab_tables = lax.all_gather(chaos_vals, MODE, axis=0, tiled=True)  32.6 us
    dot_general x3, matrix products, shards(): lax.dot_general(residual_slab, mean_inverse, (((1,), (1,)), ((), ())), pr...  29.4 us
    all_to_all x2, blocking collectives, shards(): lax.all_to_all(forcing - spatial, MODE, split_axis=0, concat_axis=1, tile...  23.5 us
    all_to_all x2, blocking collectives, shards(): lax.all_to_all(update_slab, MODE, split_axis=1, concat_axis=0, tiled=True)  23.2 us
    unnamed x46, local copies, waits for them, and re-layouts  19.5 us
    all_to_all x3, waiting for transfers between devices, shards(): lax.all_to_all(field_bf, MODE, split_axis=0, concat_axis=1, tiled=True)  16.5 us
    all_to_all x3, starting transfers between devices, shards(): lax.all_to_all(field_bf, MODE, split_axis=0, concat_axis=1, tiled=True)  16.1 us
  transfers between devices with their start and end apart: 12, of which 5 were waited for; matrix products, arithmetic and copies ran while one was open for 9% of the time, Pallas kernels for 0%

profile of v1, /device:TPU:2, one launch (start us, length us, event | category | flops | bytes accessed | tf_op | source)
XLA Modules:
  0.0 367.5 jit_solution(15394727999012768118)
XLA Ops:
  17.1 7.5 %all-to-all-start.1 = ((bf16[16,32,128]{2,1,0:T(8,128)(2,1)}), bf16[16,32,128]{2,1,0:T(8,128)(2,1)S(1)}, u32[]{:S(2)}, u32[]{:S(2)}) async-start(bf16[16,32,128]{2,1,0:T(8,128)(2,1)} %bitcast.11), calls=%async_computation.1 | async-start | bytes 262144 | tf_op jit(solution)/shard_map/all_to_all | solution.py:77
  37.7 32.6 %all-gather.2.cloned.1.call-done = bf16[128,128,128]{2,1,0:T(8,128)(2,1)} async-done(((bf16[8,128,128]{2,1,0:T(8,128)(2,1)}), bf16[128,128,128]{2,1,0:T(8,128)(2,1)}) %all-gather.2.cloned.1.call-update) | async-done | bytes 4194320 | tf_op jit(solution)/shard_map/all_gather | solution.py:54
  70.3 7.5 %convert_bitcast_fusion = bf16[16,128,16,128]{1,2,3,0:T(8,128)(2,1)} fusion(bf16[16,8,128,128]{3,2,1,0:T(8,128)(2,1)} %bitcast.203, s32[16,8]{1,0:T(8,128)S(1)} %copy.36, pred[16,8]{1,0:T(8,128)(4,1)S(1)} %iota_compare_fusion.1), kind=kOutput, calls=%fused_computation.12 | convolution fusion | flops 71307264 | bytes 12583552 | tf_op jit(solution)/shard_map/jsba,jst->jatb/dot_general | solution.py:60
  77.8 13.3 %copy.38 = bf16[16,128,16,128]{3,2,1,0:T(8,128)(2,1)} copy(bf16[16,128,16,128]{1,2,3,0:T(8,128)(2,1)} %convert_bitcast_fusion) | data formatting | bytes 16777216 | tf_op jit(solution)/shard_map/convert_element_type | solution.py:63
  91.2 9.9 %convolution_bitcast_fusion.2 = f32[4,16,8,128]{3,2,1,0:T(8,128)S(1)} fusion(bf16[2048,2048]{1,0:T(8,128)(2,1)} %param.17, bf16[256,8,16,128]{3,2,1,0:T(8,128)(2,1)} %bitcast.200, f32[16,32,128]{2,1,0:T(8,128)S(1)} %all-to-all-done, bf16[16,32,128]{2,1,0:T(8,128)(2,1)S(1)} %all-to-all-done.1), kind=kOutput, calls=%fused_computation.32 | convolution fusion | flops 537001984 | bytes 17432576 | tf_op jit(solution)/shard_map/dot_general | solution.py:83
  101.8 5.7 %all-to-all-start.2 = ((f32[32,16,128]{2,0,1:T(8,128)}), f32[32,16,128]{2,0,1:T(8,128)S(1)}, u32[]{:S(2)}, u32[]{:S(2)}) async-start(f32[32,16,128]{2,0,1:T(8,128)} %bitcast.199), calls=%async_computation.2 | async-start | bytes 524288 | tf_op jit(solution)/shard_map/all_to_all | solution.py:89
  108.2 6.6 %all-to-all-done.2 = f32[32,16,128]{2,0,1:T(8,128)S(1)} async-done(((f32[32,16,128]{2,0,1:T(8,128)}), f32[32,16,128]{2,0,1:T(8,128)S(1)}, u32[]{:S(2)}, u32[]{:S(2)}) %all-to-all-start.2) | async-done | bytes 262176 | tf_op jit(solution)/shard_map/all_to_all | solution.py:89
  117.4 17.4 %all-reduce = f32[8]{0:T(128)S(1)} all-reduce(f32[8]{0:T(128)S(1)} %dynamic-update-slice), channel_id=1, replica_groups=mesh['space_0'=8,'space_1'=2,'mode_0'=4,'mode_1'=4] {'space_0'}, use_global_device_ids=true, to_apply=%add | all-reduce | flops 8 | bytes 64
  142.4 8.6 %all-reduce.2 = f32[4]{0:T(128)S(1)} all-reduce(f32[4]{0:T(128)S(1)} %dynamic-update-slice.2), channel_id=1, replica_groups=mesh['space_0'=8,'space_1'=2,'mode_0'=4,'mode_1'=4] {'mode_0'}, use_global_device_ids=true, to_apply=%add.2 | all-reduce | flops 4 | bytes 32
  153.0 9.2 %all-reduce.3 = f32[4]{0:T(128)S(1)} all-reduce(f32[4]{0:T(128)S(1)} %dynamic-update-slice.3), channel_id=1, replica_groups=mesh['space_0'=8,'space_1'=2,'mode_0'=4,'mode_1'=4] {'mode_1'}, use_global_device_ids=true, to_apply=%add.3 | all-reduce | flops 4 | bytes 32
  177.5 6.3 %all-to-all-done.4 = bf16[16,32,128]{2,1,0:T(8,128)(2,1)S(1)} async-done(((bf16[16,32,128]{2,1,0:T(8,128)(2,1)}), bf16[16,32,128]{2,1,0:T(8,128)(2,1)S(1)}, u32[]{:S(2)}, u32[]{:S(2)}) %all-to-all-start.4) | async-done | bytes 131104 | tf_op jit(solution)/shard_map/all_to_all | solution.py:77
  183.8 11.8 %all_to_all.153 = f32[16,32,128]{2,1,0:T(8,128)S(1)} all-to-all(f32[16,32,128]{2,1,0:T(8,128)S(1)} %bitcast.204), channel_id=1, replica_groups=mesh['space_0'=8,'space_1'=2,'mode_0'=4,'mode_1'=4] {'mode_0','mode_1'}, dimensions={0} | all-to-all | bytes 524288 | tf_op jit(solution)/shard_map/all_to_all | solution.py:78
  195.6 9.8 %convolution_bitcast_fusion.1 = f32[4,16,8,128]{3,2,1,0:T(8,128)S(1)} fusion(bf16[2048,2048]{1,0:T(8,128)(2,1)} %param.17, bf16[256,8,16,128]{3,2,1,0:T(8,128)(2,1)} %bitcast.201, f32[16,32,128]{2,1,0:T(8,128)S(1)} %all_to_all.153, bf16[16,32,128]{2,1,0:T(8,128)(2,1)S(1)} %all-to-all-done.4), kind=kOutput, calls=%fused_computation.28 | convolution fusion | flops 537001984 | bytes 17432576 | tf_op jit(solution)/shard_map/dot_general | solution.py:83
  205.4 11.6 %all_to_all.154 = f32[32,16,128]{2,0,1:T(8,128)S(1)} all-to-all(f32[32,16,128]{2,0,1:T(8,128)S(1)} %bitcast.206), channel_id=1, replica_groups=mesh['space_0'=8,'space_1'=2,'mode_0'=4,'mode_1'=4] {'mode_0','mode_1'}, dimensions={1} | all-to-all | bytes 524288 | tf_op jit(solution)/shard_map/all_to_all | solution.py:89
  219.0 15.0 %all-reduce.4 = f32[8]{0:T(128)S(1)} all-reduce(f32[8]{0:T(128)S(1)} %dynamic-update-slice.4), channel_id=1, replica_groups=mesh['space_0'=8,'space_1'=2,'mode_0'=4,'mode_1'=4] {'space_0'}, use_global_device_ids=true, to_apply=%add.4 | all-reduce | flops 8 | bytes 64
  240.3 8.6 %all-reduce.6 = f32[4]{0:T(128)S(1)} all-reduce(f32[4]{0:T(128)S(1)} %dynamic-update-slice.6), channel_id=1, replica_groups=mesh['space_0'=8,'space_1'=2,'mode_0'=4,'mode_1'=4] {'mode_0'}, use_global_device_ids=true, to_apply=%add.6 | all-reduce | flops 4 | bytes 32
  250.9 9.2 %all-reduce.7 = f32[4]{0:T(128)S(1)} all-reduce(f32[4]{0:T(128)S(1)} %dynamic-update-slice.7), channel_id=1, replica_groups=mesh['space_0'=8,'space_1'=2,'mode_0'=4,'mode_1'=4] {'mode_1'}, use_global_device_ids=true, to_apply=%add.7 | all-reduce | flops 4 | bytes 32
  275.4 6.8 %all-to-all-done.7 = bf16[16,32,128]{2,1,0:T(8,128)(2,1)S(1)} async-done(((bf16[16,32,128]{2,1,0:T(8,128)(2,1)}), bf16[16,32,128]{2,1,0:T(8,128)(2,1)S(1)}, u32[]{:S(2)}, u32[]{:S(2)}) %all-to-all-start.7) | async-done | bytes 131104 | tf_op jit(solution)/shard_map/all_to_all | solution.py:77
  282.3 11.8 %all_to_all.155 = f32[16,32,128]{2,1,0:T(8,128)S(1)} all-to-all(f32[16,32,128]{2,1,0:T(8,128)S(1)} %bitcast.205), channel_id=1, replica_groups=mesh['space_0'=8,'space_1'=2,'mode_0'=4,'mode_1'=4] {'mode_0','mode_1'}, dimensions={0} | all-to-all | bytes 524288 | tf_op jit(solution)/shard_map/all_to_all | solution.py:78
  294.0 9.8 %convolution_bitcast_fusion = f32[4,16,8,128]{3,2,1,0:T(8,128)S(1)} fusion(bf16[2048,2048]{1,0:T(8,128)(2,1)} %param.17, bf16[256,8,16,128]{3,2,1,0:T(8,128)(2,1)} %bitcast.202, f32[16,32,128]{2,1,0:T(8,128)S(1)} %all_to_all.155, bf16[16,32,128]{2,1,0:T(8,128)(2,1)S(1)} %all-to-all-done.7), kind=kOutput, calls=%fused_computation.24 | convolution fusion | flops 537001984 | bytes 17432576 | tf_op jit(solution)/shard_map/dot_general | solution.py:83
  303.8 11.6 %all_to_all.156 = f32[32,16,128]{2,0,1:T(8,128)S(1)} all-to-all(f32[32,16,128]{2,0,1:T(8,128)S(1)} %bitcast.207), channel_id=1, replica_groups=mesh['space_0'=8,'space_1'=2,'mode_0'=4,'mode_1'=4] {'mode_0','mode_1'}, dimensions={1} | all-to-all | bytes 524288 | tf_op jit(solution)/shard_map/all_to_all | solution.py:89
  317.4 15.1 %all-reduce.8 = f32[8]{0:T(128)S(1)} all-reduce(f32[8]{0:T(128)S(1)} %dynamic-update-slice.8), channel_id=1, replica_groups=mesh['space_0'=8,'space_1'=2,'mode_0'=4,'mode_1'=4] {'space_0'}, use_global_device_ids=true, to_apply=%add.8 | all-reduce | flops 8 | bytes 64
  338.9 8.6 %all-reduce.10 = f32[4]{0:T(128)S(1)} all-reduce(f32[4]{0:T(128)S(1)} %dynamic-update-slice.10), channel_id=1, replica_groups=mesh['space_0'=8,'space_1'=2,'mode_0'=4,'mode_1'=4] {'mode_0'}, use_global_device_ids=true, to_apply=%add.10 | all-reduce | flops 4 | bytes 32
  349.4 9.2 %all-reduce.11 = f32[4]{0:T(128)S(1)} all-reduce(f32[4]{0:T(128)S(1)} %dynamic-update-slice.11), channel_id=1, replica_groups=mesh['space_0'=8,'space_1'=2,'mode_0'=4,'mode_1'=4] {'mode_1'}, use_global_device_ids=true, to_apply=%add.11 | all-reduce | flops 4 | bytes 32
  (111 shorter events, 88.6 us)
Async XLA Ops:
  6.5 18.1 %copy-start = (bf16[512,512]{1,0:T(8,128)(2,1)S(1)}, bf16[512,512]{1,0:T(8,128)(2,1)}, u32[]{:S(2)}) copy-start(bf16[512,512]{1,0:T(8,128)(2,1)} %param.11) | copy-start | bytes 1572868
  6.5 63.8 %all-gather.2.cloned.1.call-start = ((), (), s32[]{:S(2)}) async-start(), calls=%async_computation.9 | async-start | bytes 4456448 | tf_op jit(solution)/shard_map/all_gather | solution.py:54
  11.2 16.1 %collective-permute-start.1 = (bf16[128,128]{1,0:T(8,128)(2,1)S(1)}, bf16[128,128]{1,0:T(8,128)(2,1)S(1)}, u32[]{:S(2)}, u32[]{:S(2)}) collective-permute-start(bf16[128,128]{1,0:T(8,128)(2,1)S(1)} %gather_fusion.1), channel_id=1, source_target_pairs={{16,0},{32,16},{48,32},{64,48},{80,64},{96,80},{112,96},{128,112},... | collective-permute-start | bytes 98312 | tf_op jit(solution)/shard_map/ppermute | solution.py:24
  14.1 13.3 %collective-permute-start = (bf16[128,128]{1,0:T(8,128)(2,1)S(1)}, bf16[128,128]{1,0:T(8,128)(2,1)S(1)}, u32[]{:S(2)}, u32[]{:S(2)}) collective-permute-start(bf16[128,128]{1,0:T(8,128)(2,1)S(1)} %gather_fusion), channel_id=1, source_target_pairs={{0,16},{16,32},{32,48},{48,64},{64,80},{80,96},{96,112},{112,128},... | collective-permute-start | bytes 98312 | tf_op jit(solution)/shard_map/ppermute | solution.py:22
  17.1 15.6 %all-to-all-start.1 = ((bf16[16,32,128]{2,1,0:T(8,128)(2,1)}), bf16[16,32,128]{2,1,0:T(8,128)(2,1)S(1)}, u32[]{:S(2)}, u32[]{:S(2)}) async-start(bf16[16,32,128]{2,1,0:T(8,128)(2,1)} %bitcast.11), calls=%async_computation.1 | async-start | bytes 262144 | tf_op jit(solution)/shard_map/all_to_all | solution.py:77
  32.7 58.4 %all-to-all-start = ((f32[16,32,128]{2,1,0:T(8,128)}), f32[16,32,128]{2,1,0:T(8,128)S(1)}, u32[]{:S(2)}, u32[]{:S(2)}) async-start(f32[16,32,128]{2,1,0:T(8,128)} %bitcast.5), calls=%async_computation | async-start | bytes 524288 | tf_op jit(solution)/shard_map/all_to_all | solution.py:78
  91.1 16.4 %copy-start.3 = (f32[512,128]{1,0:T(8,128)S(1)}, f32[512,128]{1,0:T(8,128)}, u32[]{:S(2)}) copy-start(f32[512,128]{1,0:T(8,128)} %param.10) | copy-start | bytes 786436
  91.1 16.5 %copy-start.7 = (u32[256]{0:T(256)S(1)}, u32[256]{0:T(256)}, u32[]{:S(2)}) copy-start(u32[256]{0:T(256)} %constant.19) | copy-start | bytes 3076
  91.1 25.7 %copy-start.6 = (u32[256]{0:T(256)S(1)}, u32[256]{0:T(256)}, u32[]{:S(2)}) copy-start(u32[256]{0:T(256)} %constant.24) | copy-start | bytes 3076
  91.1 45.7 %copy-start.5 = (u32[256]{0:T(256)S(1)}, u32[256]{0:T(256)}, u32[]{:S(2)}) copy-start(u32[256]{0:T(256)} %constant.29) | copy-start | bytes 3076
  91.1 50.7 %copy-start.4 = (u32[256]{0:T(256)S(1)}, u32[256]{0:T(256)}, u32[]{:S(2)}) copy-start(u32[256]{0:T(256)} %constant.34) | copy-start | bytes 3076
  91.2 72.3 %copy-start.1 = (f32[512,128]{1,0:T(8,128)S(1)}, f32[512,128]{1,0:T(8,128)}, u32[]{:S(2)}) copy-start(f32[512,128]{1,0:T(8,128)} %param.9) | copy-start | bytes 786436
  91.2 86.0 %copy-start.2 = (bf16[512,256]{1,0:T(8,128)(2,1)S(1)}, bf16[512,256]{1,0:T(8,128)(2,1)}, u32[]{:S(2)}) copy-start(bf16[512,256]{1,0:T(8,128)(2,1)} %param.12) | copy-start | bytes 786436
  101.8 13.0 %all-to-all-start.2 = ((f32[32,16,128]{2,0,1:T(8,128)}), f32[32,16,128]{2,0,1:T(8,128)S(1)}, u32[]{:S(2)}, u32[]{:S(2)}) async-start(f32[32,16,128]{2,0,1:T(8,128)} %bitcast.199), calls=%async_computation.2 | async-start | bytes 524288 | tf_op jit(solution)/shard_map/all_to_all | solution.py:89
  167.3 9.9 %collective-permute-start.3 = (bf16[128,128]{1,0:T(8,128)(2,1)S(1)}, bf16[128,128]{1,0:T(8,128)(2,1)S(1)}, u32[]{:S(2)}, u32[]{:S(2)}) collective-permute-start(bf16[128,128]{1,0:T(8,128)(2,1)S(1)} %gather_fusion.3), channel_id=1, source_target_pairs={{16,0},{32,16},{48,32},{64,48},{80,64},{96,80},{112,96},{128,112},... | collective-permute-start | bytes 98312 | tf_op jit(solution)/shard_map/ppermute | solution.py:24
  168.6 8.6 %collective-permute-start.2 = (bf16[128,128]{1,0:T(8,128)(2,1)S(1)}, bf16[128,128]{1,0:T(8,128)(2,1)S(1)}, u32[]{:S(2)}, u32[]{:S(2)}) collective-permute-start(bf16[128,128]{1,0:T(8,128)(2,1)S(1)} %gather_fusion.2), channel_id=1, source_target_pairs={{0,16},{16,32},{32,48},{48,64},{64,80},{80,96},{96,112},{112,128},... | collective-permute-start | bytes 98312 | tf_op jit(solution)/shard_map/ppermute | solution.py:22
  172.8 11.0 %all-to-all-start.4 = ((bf16[16,32,128]{2,1,0:T(8,128)(2,1)}), bf16[16,32,128]{2,1,0:T(8,128)(2,1)S(1)}, u32[]{:S(2)}, u32[]{:S(2)}) async-start(bf16[16,32,128]{2,1,0:T(8,128)(2,1)} %bitcast.27), calls=%async_computation.4 | async-start | bytes 262144 | tf_op jit(solution)/shard_map/all_to_all | solution.py:77
  265.2 9.9 %collective-permute-start.5 = (bf16[128,128]{1,0:T(8,128)(2,1)S(1)}, bf16[128,128]{1,0:T(8,128)(2,1)S(1)}, u32[]{:S(2)}, u32[]{:S(2)}) collective-permute-start(bf16[128,128]{1,0:T(8,128)(2,1)S(1)} %gather_fusion.5), channel_id=1, source_target_pairs={{16,0},{32,16},{48,32},{64,48},{80,64},{96,80},{112,96},{128,112},... | collective-permute-start | bytes 98312 | tf_op jit(solution)/shard_map/ppermute | solution.py:24
  266.5 8.6 %collective-permute-start.4 = (bf16[128,128]{1,0:T(8,128)(2,1)S(1)}, bf16[128,128]{1,0:T(8,128)(2,1)S(1)}, u32[]{:S(2)}, u32[]{:S(2)}) collective-permute-start(bf16[128,128]{1,0:T(8,128)(2,1)S(1)} %gather_fusion.4), channel_id=1, source_target_pairs={{0,16},{16,32},{32,48},{48,64},{64,80},{80,96},{96,112},{112,128},... | collective-permute-start | bytes 98312 | tf_op jit(solution)/shard_map/ppermute | solution.py:22
  270.8 11.5 %all-to-all-start.7 = ((bf16[16,32,128]{2,1,0:T(8,128)(2,1)}), bf16[16,32,128]{2,1,0:T(8,128)(2,1)S(1)}, u32[]{:S(2)}, u32[]{:S(2)}) async-start(bf16[16,32,128]{2,1,0:T(8,128)(2,1)} %bitcast.38), calls=%async_computation.7 | async-start | bytes 262144 | tf_op jit(solution)/shard_map/all_to_all | solution.py:77
Sparse Core Ops, SparseCore 0:
  9.8 60.4 all-gather.1
